TPU v7x, 128 devices: a whole 4x4x4 slice. The times are simulated.
128 devices in a mesh: row: 16 (over y, x), col: 4 (over z), dp: 2 (over core).
Axes of the slice: x: 4, y: 4, z: 4, core: 2. Of those that a mesh axis runs over, the one named last changes fastest.
Arguments:
- inputs: bfloat16 [1024, 8192], P(('col', 'dp'), 'row'), may hold values from -6 to 6
- gate_weight: bfloat16 [8192, 14336], P('row', 'col'), may hold values from -0.0625 to 0.0625
- up_weight: bfloat16 [8192, 14336], P('row', 'col'), may hold values from -0.0625 to 0.0625
- down_weight: bfloat16 [14336, 8192], P('col', 'row'), may hold values from -0.046875 to 0.046875
- reward_head: bfloat16 [8192], P('row'), may hold values from -0.0625 to 0.0625
- upstream: bfloat16 [1024, 8192], P(('col', 'dp'), 'row'), may hold values from -0.59765625 to 0.59765625
- labels: int32 [1024], P(('col', 'dp')), may hold values from 0 to 1
- label_mask: int32 [1024], P(('col', 'dp')), may hold values 0 or 1
Outputs:
- gate_grad: float32 [8192, 14336], P(('row', 'dp'), 'col')
- up_grad: float32 [8192, 14336], P(('row', 'dp'), 'col')
- down_grad: float32 [14336, 8192], P(('col', 'dp'), 'row')
- input_grad: float32 [1024, 8192], P(('col', 'dp'), 'row')
All inputs are finite; a program needn't handle non-finite values. No bound on the sum of `label_mask` on one device may be relied on, other than what follows from the above.
Results may differ from a plain program's by a relative error of at most 0.035.
Values may be sent and summed in bfloat16 or wider, within the bound.
No kernel may reach another device: no remote copies, remote signals or barrier semaphores. Data moves between devices by JAX's collectives and lax.ppermute only.
A program may use at most 128 MiB of HBM per device.

v0:
```python
import jax
import jax.numpy as jnp
from jax import lax
from jax.sharding import PartitionSpec as P

reward_weight = 8.0


def transpose_product(left, right):
    return lax.dot_general(
        left, right, (((0,), (0,)), ((), ())), preferred_element_type=jnp.float32
    )


def right_transpose(left, right):
    return lax.dot_general(
        left, right, (((1,), (1,)), ((), ())), preferred_element_type=jnp.float32
    )


def gather_tokens(block):
    return lax.all_gather(block, "col", axis=0, tiled=True)


def gather_hidden(stacked):
    return lax.all_gather(stacked, "row", axis=1, tiled=True)


def column_total(term_fn, count_rows):
    return lax.psum_scatter(
        term_fn(jnp.int32(0), count_rows * lax.axis_size("col")).astype(jnp.bfloat16),
        "col",
        scatter_dimension=0,
        tiled=True,
    ).astype(jnp.float32)


def per_device(
    inputs, gate_weight, up_weight, down_weight, reward_head, upstream, labels, label_mask
):
    width = gate_weight.shape[1]
    gathered = gather_tokens(inputs)
    rows = gathered
    joined = lax.psum_scatter(
        jnp.concatenate(
            [
                jnp.dot(rows, gate_weight, preferred_element_type=jnp.float32),
                jnp.dot(rows, up_weight, preferred_element_type=jnp.float32),
            ],
            axis=1,
        ).astype(jnp.bfloat16),
        "row",
        scatter_dimension=0,
        tiled=True,
    ).astype(jnp.float32)
    gate = joined[:, :width]
    upper = joined[:, width:]
    sigmoid_gate = jax.nn.sigmoid(gate)
    hidden = (gate * sigmoid_gate * upper).astype(jnp.bfloat16)
    hidden_all = gather_hidden(hidden[None])[0]

    def output_term(start, count):
        return jnp.dot(hidden_all, down_weight, preferred_element_type=jnp.float32)

    mixed = column_total(output_term, inputs.shape[0])
    outcome = inputs.astype(jnp.float32) + mixed
    head_value = reward_head.astype(jnp.float32)
    partial_score = jnp.dot(outcome, head_value, precision=lax.Precision.HIGHEST)
    score = lax.psum(partial_score, "row")
    slope = (
        reward_weight
        * label_mask.astype(jnp.float32)
        * (jax.nn.sigmoid(score) - labels.astype(jnp.float32))
    )
    grad_out = upstream.astype(jnp.float32) + slope[:, None] * head_value[None, :]
    grad_mixed = grad_out.astype(jnp.bfloat16)
    grad_rows = gather_tokens(grad_mixed)
    rows = grad_rows
    grad_hidden = lax.psum_scatter(
        right_transpose(rows, down_weight).astype(jnp.bfloat16),
        "row",
        scatter_dimension=0,
        tiled=True,
    ).astype(jnp.float32)
    grad_gate = (grad_hidden * upper * sigmoid_gate * (1.0 + gate * (1.0 - sigmoid_gate))).astype(
        jnp.bfloat16
    )
    grad_upper = (grad_hidden * gate * sigmoid_gate).astype(jnp.bfloat16)
    grads_all = gather_hidden(jnp.stack([grad_gate, grad_upper]))

    def input_term(start, count):
        return right_transpose(grads_all[0], gate_weight) + right_transpose(grads_all[1], up_weight)

    input_grad = grad_out + column_total(input_term, inputs.shape[0])
    gate_grad, up_grad, down_grad = (
        lax.psum_scatter(
            transpose_product(gathered, grads_all[0]).astype(jnp.bfloat16),
            "dp",
            scatter_dimension=0,
            tiled=True,
        ).astype(jnp.float32),
        lax.psum_scatter(
            transpose_product(gathered, grads_all[1]).astype(jnp.bfloat16),
            "dp",
            scatter_dimension=0,
            tiled=True,
        ).astype(jnp.float32),
        lax.psum_scatter(
            transpose_product(hidden_all, grad_rows).astype(jnp.bfloat16),
            "dp",
            scatter_dimension=0,
            tiled=True,
        ).astype(jnp.float32),
    )
    return (gate_grad, up_grad, down_grad, input_grad)


def solution(mesh):
    in_specs = (
        P(("col", "dp"), "row"),
        P("row", "col"),
        P("row", "col"),
        P("col", "row"),
        P("row"),
        P(("col", "dp"), "row"),
        P(("col", "dp")),
        P(("col", "dp")),
    )
    out_specs = (
        P(("row", "dp"), "col"),
        P(("row", "dp"), "col"),
        P(("col", "dp"), "row"),
        P(("col", "dp"), "row"),
    )
    return jax.shard_map(
        per_device, mesh=mesh, in_specs=in_specs, out_specs=out_specs, check_vma=False
    )
```

profile of v0, /device:TPU:1, one launch (start us, length us, event | category | flops | bytes accessed | tf_op | source)
XLA Modules:
  0.0 488.5 jit_solution(17730826505208931112)
XLA Ops:
  7.2 13.6 %all_gather.12 = bf16[512,512]{1,0:T(8,128)(2,1)S(1)} all-gather(bf16[128,512]{1,0:T(8,128)(2,1)} %param.8), channel_id=1, replica_groups=mesh['row'=16,'col'=4,'dp'=2] {'col'}, dimensions={0}, use_global_device_ids=true | all-gather | bytes 655360 | tf_op jit(solution)/shard_map/all_gather | solution.py:22
  20.8 4.3 convolution_convert_fusion.4
  25.1 3.9 convolution_convert_fusion.5
  29.0 6.0 %pad_maximum_fusion = bf16[512,7168]{1,0:T(8,128)(2,1)} fusion(bf16[512,3584]{1,0:T(8,128)(2,1)S(1)} %convolution_convert_fusion.4, bf16[512,3584]{1,0:T(8,128)(2,1)} %convolution_convert_fusion.5), kind=kLoop, calls=%fused_computation | loop fusion | flops 14680064 | bytes 14680064 | tf_op jit(solution)/shard_map/concatenate | solution.py:45
  35.1 84.9 %reduce-scatter.8.cloned.1.call-done = bf16[32,7168]{1,0:T(8,128)(2,1)} async-done(((bf16[512,7168]{1,0:T(8,128)(2,1)}), bf16[32,7168]{1,0:T(8,128)(2,1)}) %reduce-scatter.8.cloned.1.call-update) | async-done | bytes 458768 | tf_op jit(solution)/shard_map/reduce_scatter | solution.py:44
  120.0 1.1 convert_element_type.76
  121.1 0.8 multiply_convert_fusion
  122.0 50.6 %all-gather.6.cloned.1.call-done = bf16[512,3584]{1,0:T(8,128)(2,1)} async-done(((bf16[32,3584]{1,0:T(8,128)(2,1)}), bf16[512,3584]{1,0:T(8,128)(2,1)}) %all-gather.6.cloned.1.call-update) | async-done | bytes 3670032 | tf_op jit(solution)/shard_map/all_gather | solution.py:26
  172.7 6.0 %convolution_convert_fusion.6 = bf16[512,512]{1,0:T(8,128)(2,1)} fusion(bf16[512,3584]{1,0:T(8,128)(2,1)} %all-gather.6.cloned.1.call-done, bf16[3584,512]{1,0:T(8,128)(2,1)} %param.11), kind=kOutput, calls=%fused_computation.15 | convolution fusion | flops 1879310336 | bytes 7864320 | tf_op jit(solution)/shard_map/dot_general | solution.py:63
  178.8 19.6 %reduce-scatter.10.cloned.1.call-done = bf16[128,512]{1,0:T(8,128)(2,1)} async-done(((bf16[512,512]{1,0:T(8,128)(2,1)}), bf16[128,512]{1,0:T(8,128)(2,1)}) %reduce-scatter.10.cloned.1.call-update) | async-done | bytes 131088 | tf_op jit(solution)/shard_map/reduce_scatter | solution.py:30
  198.4 1.1 convolution_bitcast_fusion
  199.5 33.2 %psum.7 = f32[128]{0:T(128)S(1)} all-reduce(f32[128]{0:T(128)S(1)} %convolution_bitcast_fusion), channel_id=1, replica_groups=mesh['row'=16,'col'=4,'dp'=2] {'row'}, use_global_device_ids=true, to_apply=%region_2.0 | all-reduce | flops 128 | bytes 1024 | tf_op jit(solution)/shard_map/psum | solution.py:69
  232.8 10.2 %all_gather.14 = bf16[512,512]{1,0:T(8,128)(2,1)S(1)} all-gather(bf16[128,512]{1,0:T(8,128)(2,1)S(1)} %fusion.14), channel_id=1, replica_groups=mesh['row'=16,'col'=4,'dp'=2] {'col'}, dimensions={0}, use_global_device_ids=true | all-gather | bytes 655360 | tf_op jit(solution)/shard_map/all_gather | solution.py:22
  243.0 6.0 %convolution_convert_fusion.3 = bf16[512,3584]{1,0:T(8,128)(2,1)} fusion(bf16[512,512]{1,0:T(8,128)(2,1)S(1)} %all_gather.14, bf16[3584,512]{1,0:T(8,128)(2,1)} %param.11), kind=kOutput, calls=%fused_computation.4 | convolution fusion | flops 1880883200 | bytes 7864320 | tf_op jit(solution)/shard_map/dot_general | solution.py:16
  249.1 81.0 %reduce-scatter.12.cloned.1.call-done = bf16[32,3584]{1,0:T(8,128)(2,1)} async-done(((bf16[512,3584]{1,0:T(8,128)(2,1)}), bf16[32,3584]{1,0:T(8,128)(2,1)}) %reduce-scatter.12.cloned.1.call-update) | async-done | bytes 229392 | tf_op jit(solution)/shard_map/reduce_scatter | solution.py:79
  330.0 1.2 fusion.16
  331.2 0.8 pad_maximum_fusion.1
  332.1 6.0 %convolution_convert_fusion = bf16[3584,512]{1,0:T(8,128)(2,1)} fusion(bf16[512,3584]{1,0:T(8,128)(2,1)} %all-gather.6.cloned.1.call-done, bf16[512,512]{1,0:T(8,128)(2,1)S(1)} %all_gather.14), kind=kOutput, calls=%fused_computation.1 | convolution fusion | flops 1880883200 | bytes 7864320 | tf_op jit(solution)/shard_map/dot_general | solution.py:10
  338.1 61.8 %all-gather.4.cloned.1.call-done = bf16[2,512,3584]{2,1,0:T(8,128)(2,1)} async-done(((bf16[2,32,3584]{2,1,0:T(8,128)(2,1)}), bf16[2,512,3584]{2,1,0:T(8,128)(2,1)}) %all-gather.4.cloned.1.call-update) | async-done | bytes 7340048 | tf_op jit(solution)/shard_map/all_gather | solution.py:26
  399.9 5.4 %fusion.2 = f32[512,512]{1,0:T(8,128)S(1)} fusion(bf16[512,3584]{1,0:T(8,128)(2,1)} %param.9, bf16[2,512,3584]{2,1,0:T(8,128)(2,1)} %all-gather.4.cloned.1.call-done), kind=kOutput, calls=%fused_computation.11 | convolution fusion | flops 1879048192 | bytes 8388608 | tf_op jit(solution)/shard_map/dot_general | solution.py:16
  405.3 0.9 copy-done.7
  406.1 2.9 fusion.5
  409.1 0.2 reduce-scatter.16.cloned.1.call-start
  409.3 6.0 %fusion.1 = bf16[512,3584]{0,1:T(8,128)(2,1)} fusion(bf16[512,512]{1,0:T(8,128)(2,1)S(1)} %all_gather.12, bf16[2,512,3584]{2,1,0:T(8,128)(2,1)} %all-gather.4.cloned.1.call-done), kind=kOutput, calls=%fused_computation.8 | convolution fusion | flops 1880883200 | bytes 7864320 | tf_op jit(solution)/shard_map/dot_general | solution.py:10
  415.4 6.3 %fusion = bf16[512,3584]{0,1:T(8,128)(2,1)} fusion(bf16[512,512]{1,0:T(8,128)(2,1)S(1)} %all_gather.12, bf16[2,512,3584]{2,1,0:T(8,128)(2,1)} %all-gather.4.cloned.1.call-done), kind=kOutput, calls=%fused_computation.7 | convolution fusion | flops 1880883200 | bytes 7864320 | tf_op jit(solution)/shard_map/dot_general | solution.py:10
  421.7 3.9 convert_element_type.94
  425.5 14.9 %reduce-scatter.20.cloned.1.call-done = bf16[128,512]{1,0:T(8,128)(2,1)} async-done(((bf16[512,512]{1,0:T(8,128)(2,1)}), bf16[128,512]{1,0:T(8,128)(2,1)}) %reduce-scatter.20.cloned.1.call-update) | async-done | bytes 131088 | tf_op jit(solution)/shard_map/reduce_scatter | solution.py:30
  440.5 1.7 convert_add_fusion
  442.2 17.1 %reduce-scatter.16.cloned.1.call-done = bf16[256,3584]{0,1:T(8,128)(2,1)} async-done(((bf16[512,3584]{0,1:T(8,128)(2,1)}), bf16[256,3584]{0,1:T(8,128)(2,1)}) %reduce-scatter.16.cloned.1.call-update) | async-done | bytes 1835024 | tf_op jit(solution)/shard_map/reduce_scatter | solution.py:102
  459.3 4.0 copy.13
  463.3 14.7 %reduce-scatter.14.cloned.1.call-done = bf16[256,3584]{0,1:T(8,128)(2,1)} async-done(((bf16[512,3584]{0,1:T(8,128)(2,1)}), bf16[256,3584]{0,1:T(8,128)(2,1)}) %reduce-scatter.14.cloned.1.call-update) | async-done | bytes 1835024 | tf_op jit(solution)/shard_map/reduce_scatter | solution.py:96
  478.0 4.0 copy.12
  (37 shorter events, 0.7 us)
Async XLA Ops:
  7.2 112.8 %reduce-scatter.8.cloned.1.call-start = ((), (), s32[]{:S(2)}) async-start(), calls=%async_computation.7 | async-start | bytes 7798784 | tf_op jit(solution)/shard_map/reduce_scatter | solution.py:44
  20.8 4.3 copy-start.6
  35.0 137.6 %all-gather.6.cloned.1.call-start = ((), (), s32[]{:S(2)}) async-start(), calls=%async_computation.15 | async-start | bytes 3899392 | tf_op jit(solution)/shard_map/all_gather | solution.py:26
  121.9 56.8 %copy-start.2 = (bf16[512]{0:T(512)(128)(2,1)S(1)}, bf16[512]{0:T(512)(128)(2,1)}, u32[]{:S(2)}) copy-start(bf16[512]{0:T(512)(128)(2,1)} %param.12) | copy-start | bytes 3076
  121.9 76.5 %copy-start = (bf16[128,512]{1,0:T(8,128)(2,1)S(1)}, bf16[128,512]{1,0:T(8,128)(2,1)}, u32[]{:S(2)}) copy-start(bf16[128,512]{1,0:T(8,128)(2,1)} %param.8) | copy-start | bytes 393220
  122.0 110.7 %copy-start.3 = (s32[128]{0:T(128)S(1)}, s32[128]{0:T(128)}, u32[]{:S(2)}) copy-start(s32[128]{0:T(128)} %param.14) | copy-start | bytes 1540
  122.0 110.7 %copy-start.4 = (s32[128]{0:T(128)S(1)}, s32[128]{0:T(128)}, u32[]{:S(2)}) copy-start(s32[128]{0:T(128)} %param.15) | copy-start | bytes 1540
  122.0 110.7 %copy-start.1 = (bf16[128,512]{1,0:T(8,128)(2,1)S(1)}, bf16[128,512]{1,0:T(8,128)(2,1)}, u32[]{:S(2)}) copy-start(bf16[128,512]{1,0:T(8,128)(2,1)} %param.13) | copy-start | bytes 393220
  122.0 76.4 %reduce-scatter.10.cloned.1.call-start = ((), (), s32[]{:S(2)}) async-start(), calls=%async_computation.8 | async-start | bytes 655360 | tf_op jit(solution)/shard_map/reduce_scatter | solution.py:30
  178.7 151.3 %reduce-scatter.12.cloned.1.call-start = ((), (), s32[]{:S(2)}) async-start(), calls=%async_computation.9 | async-start | bytes 3899392 | tf_op jit(solution)/shard_map/reduce_scatter | solution.py:79
  249.0 150.9 %all-gather.4.cloned.1.call-start = ((), (), s32[]{:S(2)}) async-start(), calls=%async_computation.10 | async-start | bytes 7798784 | tf_op jit(solution)/shard_map/all_gather | solution.py:26
  332.0 89.7 %reduce-scatter.18.cloned.1.call-start = ((), (), s32[]{:S(2)}) async-start(), calls=%async_computation.13 | async-start | bytes 5505024 | tf_op jit(solution)/shard_map/reduce_scatter | solution.py:108
  338.1 102.4 %reduce-scatter.20.cloned.1.call-start = ((), (), s32[]{:S(2)}) async-start(), calls=%async_computation.14 | async-start | bytes 655360 | tf_op jit(solution)/shard_map/reduce_scatter | solution.py:30
  399.9 5.4 %copy-start.5 = (bf16[2,512,3584]{2,1,0:T(8,128)(2,1)S(1)}, bf16[2,512,3584]{2,1,0:T(8,128)(2,1)}, u32[]{:S(2)}) copy-start(bf16[2,512,3584]{2,1,0:T(8,128)(2,1)} %all-gather.4.cloned.1.call-done) | copy-start | bytes 22020100
  399.9 6.3 %copy-start.7 = (bf16[512,3584]{1,0:T(8,128)(2,1)S(1)}, bf16[512,3584]{1,0:T(8,128)(2,1)}, u32[]{:S(2)}) copy-start(bf16[512,3584]{1,0:T(8,128)(2,1)} %param.10) | copy-start | bytes 11010052
  409.1 50.3 %reduce-scatter.16.cloned.1.call-start = ((), (), s32[]{:S(2)}) async-start(), calls=%async_computation.12 | async-start | bytes 5505024 | tf_op jit(solution)/shard_map/reduce_scatter | solution.py:102
  415.3 62.7 %reduce-scatter.14.cloned.1.call-start = ((), (), s32[]{:S(2)}) async-start(), calls=%async_computation.11 | async-start | bytes 5505024 | tf_op jit(solution)/shard_map/reduce_scatter | solution.py:96
Sparse Core Ops, SparseCore 0:
  35.1 84.8 reduce-scatter.7
  122.9 49.6 all-gather.5
  178.8 19.5 reduce-scatter.9
  249.1 80.8 reduce-scatter.11
  332.8 67.0 all-gather.3
  402.8 14.3 reduce-scatter.17
  419.6 20.8 reduce-scatter.19
  443.4 15.8 reduce-scatter.15
  462.4 15.5 reduce-scatter.13
where the time goes:
time: 489 us; the launch traced here: 488 us
  waiting for transfers between devices  345 us (71%)
  blocking collectives  56.9 us (12%)
  matrix products  47.8 us (10%)
  other arithmetic  15.5 us (3%)
  between operations  14 us (3%)
  local copies, waits for them, and re-layouts  8.87 us (2%)
    all_gather x2, waiting for transfers between devices, gather_hidden(): return lax.all_gather(stacked, 'row', axis=1, tiled=True)  112 us
    reduce_scatter x1, waiting for transfers between devices, per_device(): lax.psum_scatter(jnp.concatenate([jnp.dot(rows, gate_weight, preferred_el...  84.9 us
    reduce_scatter x1, waiting for transfers between devices, per_device(): lax.psum_scatter(right_transpose(rows, down_weight).astype(jnp.bfloat16),...  81 us
    reduce_scatter x2, waiting for transfers between devices, column_total(): lax.psum_scatter(term_fn(jnp.int32(0), count_rows * lax.axis_size('col'))...  34.6 us
    psum x1, blocking collectives, per_device(): score = lax.psum(partial_score, 'row')  33.2 us
    all_gather x2, blocking collectives, gather_tokens(): return lax.all_gather(block, 'col', axis=0, tiled=True)  23.8 us
    dot_general x3, matrix products, transpose_product(): lax.dot_general(left, right, (((0,), (0,)), ((), ())), preferred_element_...  18.2 us
    reduce_scatter x1, waiting for transfers between devices, per_device(): lax.psum_scatter(transpose_product(gathered, grads_all[1]).astype(jnp.bfl...  17.1 us
  transfers between devices with their start and end apart: 9, of which 8 were waited for; matrix products, arithmetic and copies ran while one was open for 7% of the time, Pallas kernels for 0%

commit v1 on v0

--- a/solution.py
+++ b/solution.py
@@ -4,6 +4,22 @@
 from jax.sharding import PartitionSpec as P
 
 reward_weight = 8.0
+
+
+def collect(x, axis, dim):
+    ways, here, step = (lax.axis_size(axis), lax.axis_index(axis), x.shape[dim])
+    shape = [n * ways if d == dim else n for d, n in enumerate(x.shape)]
+    full = lax.dynamic_update_slice_in_dim(jnp.zeros(shape, x.dtype), x, here * step, axis=dim)
+    going_up = going_down = x
+    for far in range(1, ways // 2 + 1):
+        going_up = lax.ppermute(going_up, axis, [(d, (d + 1) % ways) for d in range(ways)])
+        full = lax.dynamic_update_slice_in_dim(full, going_up, (here - far) % ways * step, axis=dim)
+        if 2 * far < ways:
+            going_down = lax.ppermute(going_down, axis, [(d, (d - 1) % ways) for d in range(ways)])
+            full = lax.dynamic_update_slice_in_dim(
+                full, going_down, (here + far) % ways * step, axis=dim
+            )
+    return full
 
 
 def transpose_product(left, right):
@@ -23,7 +39,7 @@
 
 
 def gather_hidden(stacked):
-    return lax.all_gather(stacked, "row", axis=1, tiled=True)
+    return collect(stacked, "row", 1)
 
 
 def column_total(term_fn, count_rows):

time: 489 us -> 545 us (1.11)
  starting transfers between devices: 0.55 us -> 71.1 us
  waiting for transfers between devices: 345 us -> 302 us
  local copies, waits for them, and re-layouts: 8.87 us -> 36.1 us
    all_gather x2 -> x0, waiting for transfers between devices: 112 us -> none  [gather_hidden(): return lax.all_gather(stacked, 'row', axis=1, tiled=True)]
    ppermute x0 -> x30, starting transfers between devices: none -> 70.8 us  [the longest x14 68.8 us: collect(): lax.ppermute(going_down, axis, [(d, (d - 1) % ways) for d in range(ways)])]
    ppermute x0 -> x30, waiting for transfers between devices: none -> 68.2 us  [the longest x16 37.4 us: collect(): lax.ppermute(going_up, axis, [(d, (d + 1) % ways) for d in range(ways)])]
    dynamic_update_slice x0 -> x30, local copies, waits for them, and re-layouts: none -> 22.7 us  [the longest x16 12.1 us: collect(): lax.dynamic_update_slice_in_dim(full, going_up, (here - far) % ways * ste...]
  transfers between devices with their start and end apart: 9 -> 37, of which waited for: 8 -> 26; matrix products, arithmetic and copies ran while one was open for 7% -> 11% of each run, Pallas kernels for 0% -> 0%
where the time goes in v1:
time: 545 us; the launch traced here: 544 us
  waiting for transfers between devices  302 us (55%)
  starting transfers between devices  71.1 us (13%)
  blocking collectives  57.1 us (10%)
  matrix products  47.5 us (9%)
  local copies, waits for them, and re-layouts  36.1 us (7%)
  other arithmetic  15.5 us (3%)
  between operations  14.3 us (3%)
    reduce_scatter x1, waiting for transfers between devices, per_device(): lax.psum_scatter(jnp.concatenate([jnp.dot(rows, gate_weight, preferred_el...  84.9 us
    reduce_scatter x1, waiting for transfers between devices, per_device(): lax.psum_scatter(right_transpose(rows, down_weight).astype(jnp.bfloat16),...  81 us
    ppermute x14, starting transfers between devices, collect(): lax.ppermute(going_down, axis, [(d, (d - 1) % ways) for d in range(ways)])  68.8 us
    ppermute x16, waiting for transfers between devices, collect(): lax.ppermute(going_up, axis, [(d, (d + 1) % ways) for d in range(ways)])  37.4 us
    reduce_scatter x2, waiting for transfers between devices, column_total(): lax.psum_scatter(term_fn(jnp.int32(0), count_rows * lax.axis_size('col'))...  36.4 us
    psum x1, blocking collectives, per_device(): score = lax.psum(partial_score, 'row')  33.1 us
    ppermute x14, waiting for transfers between devices, collect(): lax.ppermute(going_down, axis, [(d, (d - 1) % ways) for d in range(ways)])  30.9 us
    all_gather x2, blocking collectives, gather_tokens(): return lax.all_gather(block, 'col', axis=0, tiled=True)  24 us
  transfers between devices with their start and end apart: 37, of which 26 were waited for; matrix products, arithmetic and copies ran while one was open for 11% of the time, Pallas kernels for 0%

profile of v1, /device:TPU:1, one launch (start us, length us, event | category | flops | bytes accessed | tf_op | source)
XLA Modules:
  0.0 544.0 jit_solution(7773975374798200609)
XLA Ops:
  7.2 13.6 %all_gather.6 = bf16[512,512]{1,0:T(8,128)(2,1)S(1)} all-gather(bf16[128,512]{1,0:T(8,128)(2,1)} %param.8), channel_id=1, replica_groups=mesh['row'=16,'col'=4,'dp'=2] {'col'}, dimensions={0}, use_global_device_ids=true | all-gather | bytes 655360 | tf_op jit(solution)/shard_map/all_gather | solution.py:38
  29.0 5.9 %pad_maximum_fusion = bf16[512,7168]{1,0:T(8,128)(2,1)} fusion(bf16[512,3584]{1,0:T(8,128)(2,1)S(1)} %convolution_convert_fusion.4, bf16[512,3584]{1,0:T(8,128)(2,1)} %convolution_convert_fusion.5), kind=kLoop, calls=%fused_computation | loop fusion | flops 14680064 | bytes 14680064 | tf_op jit(solution)/shard_map/concatenate | solution.py:61
  35.0 84.9 %reduce-scatter.8.cloned.1.call-done = bf16[32,7168]{1,0:T(8,128)(2,1)} async-done(((bf16[512,7168]{1,0:T(8,128)(2,1)}), bf16[32,7168]{1,0:T(8,128)(2,1)}) %reduce-scatter.8.cloned.1.call-update) | async-done | bytes 458768 | tf_op jit(solution)/shard_map/reduce_scatter | solution.py:60
  132.5 4.8 collective-permute-start.3
  140.7 4.8 collective-permute-start.5
  148.8 4.8 collective-permute-start.7
  165.2 4.9 collective-permute-start.11
  174.4 5.1 collective-permute-start.13
  186.1 8.7 %collective-permute-done.14 = bf16[1,32,3584]{2,1,0:T(8,128)(2,1)S(1)} collective-permute-done((bf16[1,32,3584]{2,1,0:T(8,128)(2,1)S(1)}, bf16[1,32,3584]{2,1,0:T(8,128)(2,1)S(1)}, u32[]{:S(2)}, u32[]{:S(2)}) %collective-permute-start.14) | collective-permute-done | bytes 229408 | tf_op jit(solution)/shard_map/ppermute | solution.py:15
  195.6 5.0 convolution_convert_fusion.6
  200.7 26.2 %reduce-scatter.10.cloned.1.call-done = bf16[128,512]{1,0:T(8,128)(2,1)} async-done(((bf16[512,512]{1,0:T(8,128)(2,1)}), bf16[128,512]{1,0:T(8,128)(2,1)}) %reduce-scatter.10.cloned.1.call-update) | async-done | bytes 131088 | tf_op jit(solution)/shard_map/reduce_scatter | solution.py:46
  228.0 33.1 %psum.7 = f32[128]{0:T(128)S(1)} all-reduce(f32[128]{0:T(128)S(1)} %convolution_bitcast_fusion), channel_id=1, replica_groups=mesh['row'=16,'col'=4,'dp'=2] {'row'}, use_global_device_ids=true, to_apply=%region_2.3 | all-reduce | flops 128 | bytes 1024 | tf_op jit(solution)/shard_map/psum | solution.py:85
  261.3 10.4 %all_gather.7 = bf16[512,512]{1,0:T(8,128)(2,1)S(1)} all-gather(bf16[128,512]{1,0:T(8,128)(2,1)S(1)} %fusion.14), channel_id=1, replica_groups=mesh['row'=16,'col'=4,'dp'=2] {'col'}, dimensions={0}, use_global_device_ids=true | all-gather | bytes 655360 | tf_op jit(solution)/shard_map/all_gather | solution.py:38
  271.7 6.0 %convolution_convert_fusion.3 = bf16[512,3584]{1,0:T(8,128)(2,1)} fusion(bf16[512,512]{1,0:T(8,128)(2,1)S(1)} %all_gather.7, bf16[3584,512]{1,0:T(8,128)(2,1)} %param.11), kind=kOutput, calls=%fused_computation.4 | convolution fusion | flops 1880883200 | bytes 7864320 | tf_op jit(solution)/shard_map/dot_general | solution.py:32
  277.7 81.0 %reduce-scatter.12.cloned.1.call-done = bf16[32,3584]{1,0:T(8,128)(2,1)} async-done(((bf16[512,3584]{1,0:T(8,128)(2,1)}), bf16[32,3584]{1,0:T(8,128)(2,1)}) %reduce-scatter.12.cloned.1.call-update) | async-done | bytes 229392 | tf_op jit(solution)/shard_map/reduce_scatter | solution.py:95
  365.1 6.1 %convolution_convert_fusion = bf16[3584,512]{1,0:T(8,128)(2,1)} fusion(bf16[512,3584]{1,0:T(8,128)(2,1)} %bitcast_dynamic-update-slice_fusion, bf16[512,512]{1,0:T(8,128)(2,1)S(1)} %all_gather.7), kind=kOutput, calls=%fused_computation.1 | convolution fusion | flops 1880883200 | bytes 7864320 | tf_op jit(solution)/shard_map/dot_general | solution.py:26
  382.3 5.5 %collective-permute-start.18 = (bf16[2,32,3584]{2,1,0:T(8,128)(2,1)S(1)}, bf16[2,32,3584]{2,1,0:T(8,128)(2,1)S(1)}, u32[]{:S(2)}, u32[]{:S(2)}) collective-permute-start(bf16[2,32,3584]{2,1,0:T(8,128)(2,1)S(1)} %collective-permute-done.16), channel_id=1, source_target_pairs={{0,120},{8,0},{16,8},{24,16},{32,24},{40,32},{48,40},{56,48},{64,5... | collective-permute-start | bytes 1376264 | tf_op jit(solution)/shard_map/ppermute | solution.py:18
  389.1 4.9 collective-permute-done.18
  394.0 5.5 %collective-permute-start.20 = (bf16[2,32,3584]{2,1,0:T(8,128)(2,1)S(1)}, bf16[2,32,3584]{2,1,0:T(8,128)(2,1)S(1)}, u32[]{:S(2)}, u32[]{:S(2)}) collective-permute-start(bf16[2,32,3584]{2,1,0:T(8,128)(2,1)S(1)} %collective-permute-done.18), channel_id=1, source_target_pairs={{0,120},{8,0},{16,8},{24,16},{32,24},{40,32},{48,40},{56,48},{64,5... | collective-permute-start | bytes 1376264 | tf_op jit(solution)/shard_map/ppermute | solution.py:18
  405.0 5.2 collective-permute-start.22
  415.6 5.2 collective-permute-start.24
  426.6 5.2 collective-permute-start.26
  433.8 4.9 collective-permute-done.26
  438.7 5.2 collective-permute-start.28
  447.0 4.9 collective-permute-done.28
  452.7 6.9 %collective-permute-done.29 = bf16[2,32,3584]{2,1,0:T(8,128)(2,1)S(1)} collective-permute-done((bf16[2,32,3584]{2,1,0:T(8,128)(2,1)S(1)}, bf16[2,32,3584]{2,1,0:T(8,128)(2,1)S(1)}, u32[]{:S(2)}, u32[]{:S(2)}) %collective-permute-start.29) | collective-permute-done | bytes 458784 | tf_op jit(solution)/shard_map/ppermute | solution.py:15
  464.7 4.9 fusion.5
  469.7 6.0 %fusion.1 = bf16[512,3584]{0,1:T(8,128)(2,1)} fusion(bf16[512,512]{1,0:T(8,128)(2,1)S(1)} %all_gather.6, bf16[2,512,3584]{2,1,0:T(8,128)(2,1)} %constant_dynamic-update-slice_fusion), kind=kOutput, calls=%fused_computation.8 | convolution fusion | flops 1880883200 | bytes 7864320 | tf_op jit(solution)/shard_map/dot_general | solution.py:26
  475.8 6.0 %fusion = bf16[512,3584]{0,1:T(8,128)(2,1)} fusion(bf16[512,512]{1,0:T(8,128)(2,1)S(1)} %all_gather.6, bf16[2,512,3584]{2,1,0:T(8,128)(2,1)} %constant_dynamic-update-slice_fusion), kind=kOutput, calls=%fused_computation.7 | convolution fusion | flops 1880883200 | bytes 7864320 | tf_op jit(solution)/shard_map/dot_general | solution.py:26
  485.7 10.1 %reduce-scatter.20.cloned.1.call-done = bf16[128,512]{1,0:T(8,128)(2,1)} async-done(((bf16[512,512]{1,0:T(8,128)(2,1)}), bf16[128,512]{1,0:T(8,128)(2,1)}) %reduce-scatter.20.cloned.1.call-update) | async-done | bytes 131088 | tf_op jit(solution)/shard_map/reduce_scatter | solution.py:46
  497.5 17.0 %reduce-scatter.16.cloned.1.call-done = bf16[256,3584]{0,1:T(8,128)(2,1)} async-done(((bf16[512,3584]{0,1:T(8,128)(2,1)}), bf16[256,3584]{0,1:T(8,128)(2,1)}) %reduce-scatter.16.cloned.1.call-update) | async-done | bytes 1835024 | tf_op jit(solution)/shard_map/reduce_scatter | solution.py:118
  518.5 14.7 %reduce-scatter.14.cloned.1.call-done = bf16[256,3584]{0,1:T(8,128)(2,1)} async-done(((bf16[512,3584]{0,1:T(8,128)(2,1)}), bf16[256,3584]{0,1:T(8,128)(2,1)}) %reduce-scatter.14.cloned.1.call-update) | async-done | bytes 1835024 | tf_op jit(solution)/shard_map/reduce_scatter | solution.py:112
  (125 shorter events, 112.0 us)
Async XLA Ops:
  7.2 112.8 %reduce-scatter.8.cloned.1.call-start = ((), (), s32[]{:S(2)}) async-start(), calls=%async_computation.7 | async-start | bytes 7798784 | tf_op jit(solution)/shard_map/reduce_scatter | solution.py:60
  35.0 191.9 %reduce-scatter.10.cloned.1.call-start = ((), (), s32[]{:S(2)}) async-start(), calls=%async_computation.8 | async-start | bytes 655360 | tf_op jit(solution)/shard_map/reduce_scatter | solution.py:46
  123.9 8.5 %collective-permute-start = (bf16[1,32,3584]{2,1,0:T(8,128)(2,1)S(1)}, bf16[1,32,3584]{2,1,0:T(8,128)(2,1)S(1)}, u32[]{:S(2)}, u32[]{:S(2)}) collective-permute-start(bf16[1,32,3584]{2,1,0:T(8,128)(2,1)S(1)} %bitcast.68), channel_id=1, source_target_pairs={{0,8},{8,16},{16,24},{24,32},{32,40},{40,48},{48,56},{56,64},{64,7... | collective-permute-start | bytes 688136 | tf_op jit(solution)/shard_map/ppermute | solution.py:15
  132.5 8.2 %collective-permute-start.2 = (bf16[1,32,3584]{2,1,0:T(8,128)(2,1)S(1)}, bf16[1,32,3584]{2,1,0:T(8,128)(2,1)S(1)}, u32[]{:S(2)}, u32[]{:S(2)}) collective-permute-start(bf16[1,32,3584]{2,1,0:T(8,128)(2,1)S(1)} %collective-permute-done), channel_id=1, source_target_pairs={{0,8},{8,16},{16,24},{24,32},{32,40},{40,48},{48,56},{56,64},{64,7... | collective-permute-start | bytes 688136 | tf_op jit(solution)/shard_map/ppermute | solution.py:15
  132.5 8.2 %collective-permute-start.3 = (bf16[1,32,3584]{2,1,0:T(8,128)(2,1)S(1)}, bf16[1,32,3584]{2,1,0:T(8,128)(2,1)S(1)}, u32[]{:S(2)}, u32[]{:S(2)}) collective-permute-start(bf16[1,32,3584]{2,1,0:T(8,128)(2,1)S(1)} %collective-permute-done.1), channel_id=1, source_target_pairs={{0,120},{8,0},{16,8},{24,16},{32,24},{40,32},{48,40},{56,48},{64,5... | collective-permute-start | bytes 688136 | tf_op jit(solution)/shard_map/ppermute | solution.py:18
  140.6 8.2 %collective-permute-start.4 = (bf16[1,32,3584]{2,1,0:T(8,128)(2,1)S(1)}, bf16[1,32,3584]{2,1,0:T(8,128)(2,1)S(1)}, u32[]{:S(2)}, u32[]{:S(2)}) collective-permute-start(bf16[1,32,3584]{2,1,0:T(8,128)(2,1)S(1)} %collective-permute-done.2), channel_id=1, source_target_pairs={{0,8},{8,16},{16,24},{24,32},{32,40},{40,48},{48,56},{56,64},{64,7... | collective-permute-start | bytes 688136 | tf_op jit(solution)/shard_map/ppermute | solution.py:15
  140.7 8.2 %collective-permute-start.5 = (bf16[1,32,3584]{2,1,0:T(8,128)(2,1)S(1)}, bf16[1,32,3584]{2,1,0:T(8,128)(2,1)S(1)}, u32[]{:S(2)}, u32[]{:S(2)}) collective-permute-start(bf16[1,32,3584]{2,1,0:T(8,128)(2,1)S(1)} %collective-permute-done.3), channel_id=1, source_target_pairs={{0,120},{8,0},{16,8},{24,16},{32,24},{40,32},{48,40},{56,48},{64,5... | collective-permute-start | bytes 688136 | tf_op jit(solution)/shard_map/ppermute | solution.py:18
  165.2 9.2 %collective-permute-start.10 = (bf16[1,32,3584]{2,1,0:T(8,128)(2,1)S(1)}, bf16[1,32,3584]{2,1,0:T(8,128)(2,1)S(1)}, u32[]{:S(2)}, u32[]{:S(2)}) collective-permute-start(bf16[1,32,3584]{2,1,0:T(8,128)(2,1)S(1)} %collective-permute-done.8), channel_id=1, source_target_pairs={{0,8},{8,16},{16,24},{24,32},{32,40},{40,48},{48,56},{56,64},{64,7... | collective-permute-start | bytes 688136 | tf_op jit(solution)/shard_map/ppermute | solution.py:15
  165.2 9.2 %collective-permute-start.11 = (bf16[1,32,3584]{2,1,0:T(8,128)(2,1)S(1)}, bf16[1,32,3584]{2,1,0:T(8,128)(2,1)S(1)}, u32[]{:S(2)}, u32[]{:S(2)}) collective-permute-start(bf16[1,32,3584]{2,1,0:T(8,128)(2,1)S(1)} %collective-permute-done.9), channel_id=1, source_target_pairs={{0,120},{8,0},{16,8},{24,16},{32,24},{40,32},{48,40},{56,48},{64,5... | collective-permute-start | bytes 688136 | tf_op jit(solution)/shard_map/ppermute | solution.py:18
  174.4 10.3 %collective-permute-start.12 = (bf16[1,32,3584]{2,1,0:T(8,128)(2,1)S(1)}, bf16[1,32,3584]{2,1,0:T(8,128)(2,1)S(1)}, u32[]{:S(2)}, u32[]{:S(2)}) collective-permute-start(bf16[1,32,3584]{2,1,0:T(8,128)(2,1)S(1)} %collective-permute-done.10), channel_id=1, source_target_pairs={{0,8},{8,16},{16,24},{24,32},{32,40},{40,48},{48,56},{56,64},{64,7... | collective-permute-start | bytes 688136 | tf_op jit(solution)/shard_map/ppermute | solution.py:15
  174.4 11.0 %collective-permute-start.13 = (bf16[1,32,3584]{2,1,0:T(8,128)(2,1)S(1)}, bf16[1,32,3584]{2,1,0:T(8,128)(2,1)S(1)}, u32[]{:S(2)}, u32[]{:S(2)}) collective-permute-start(bf16[1,32,3584]{2,1,0:T(8,128)(2,1)S(1)} %collective-permute-done.11), channel_id=1, source_target_pairs={{0,120},{8,0},{16,8},{24,16},{32,24},{40,32},{48,40},{56,48},{64,5... | collective-permute-start | bytes 688136 | tf_op jit(solution)/shard_map/ppermute | solution.py:18
  184.7 10.1 %collective-permute-start.14 = (bf16[1,32,3584]{2,1,0:T(8,128)(2,1)S(1)}, bf16[1,32,3584]{2,1,0:T(8,128)(2,1)S(1)}, u32[]{:S(2)}, u32[]{:S(2)}) collective-permute-start(bf16[1,32,3584]{2,1,0:T(8,128)(2,1)S(1)} %collective-permute-done.12), channel_id=1, source_target_pairs={{0,8},{8,16},{16,24},{24,32},{32,40},{40,48},{48,56},{56,64},{64,7... | collective-permute-start | bytes 688136 | tf_op jit(solution)/shard_map/ppermute | solution.py:15
  200.6 158.2 %reduce-scatter.12.cloned.1.call-start = ((), (), s32[]{:S(2)}) async-start(), calls=%async_computation.9 | async-start | bytes 3899392 | tf_op jit(solution)/shard_map/reduce_scatter | solution.py:95
  277.7 204.2 %reduce-scatter.18.cloned.1.call-start = ((), (), s32[]{:S(2)}) async-start(), calls=%async_computation.12 | async-start | bytes 5505024 | tf_op jit(solution)/shard_map/reduce_scatter | solution.py:124
  364.1 13.0 %collective-permute-start.15 = (bf16[2,32,3584]{2,1,0:T(8,128)(2,1)S(1)}, bf16[2,32,3584]{2,1,0:T(8,128)(2,1)S(1)}, u32[]{:S(2)}, u32[]{:S(2)}) collective-permute-start(bf16[2,32,3584]{2,1,0:T(8,128)(2,1)S(1)} %get-tuple-element.12), channel_id=1, source_target_pairs={{0,8},{8,16},{16,24},{24,32},{32,40},{40,48},{48,56},{56,64},{64,7... | collective-permute-start | bytes 1376264 | tf_op jit(solution)/shard_map/ppermute | solution.py:15
  371.2 124.6 %reduce-scatter.20.cloned.1.call-start = ((), (), s32[]{:S(2)}) async-start(), calls=%async_computation.13 | async-start | bytes 655360 | tf_op jit(solution)/shard_map/reduce_scatter | solution.py:46
  371.2 11.0 %collective-permute-start.16 = (bf16[2,32,3584]{2,1,0:T(8,128)(2,1)S(1)}, bf16[2,32,3584]{2,1,0:T(8,128)(2,1)S(1)}, u32[]{:S(2)}, u32[]{:S(2)}) collective-permute-start(bf16[2,32,3584]{2,1,0:T(8,128)(2,1)S(1)} %get-tuple-element.12), channel_id=1, source_target_pairs={{0,120},{8,0},{16,8},{24,16},{32,24},{40,32},{48,40},{56,48},{64,5... | collective-permute-start | bytes 1376264 | tf_op jit(solution)/shard_map/ppermute | solution.py:18
  377.1 12.0 %collective-permute-start.17 = (bf16[2,32,3584]{2,1,0:T(8,128)(2,1)S(1)}, bf16[2,32,3584]{2,1,0:T(8,128)(2,1)S(1)}, u32[]{:S(2)}, u32[]{:S(2)}) collective-permute-start(bf16[2,32,3584]{2,1,0:T(8,128)(2,1)S(1)} %collective-permute-done.15), channel_id=1, source_target_pairs={{0,8},{8,16},{16,24},{24,32},{32,40},{40,48},{48,56},{56,64},{64,7... | collective-permute-start | bytes 1376264 | tf_op jit(solution)/shard_map/ppermute | solution.py:15
  382.3 11.8 %collective-permute-start.18 = (bf16[2,32,3584]{2,1,0:T(8,128)(2,1)S(1)}, bf16[2,32,3584]{2,1,0:T(8,128)(2,1)S(1)}, u32[]{:S(2)}, u32[]{:S(2)}) collective-permute-start(bf16[2,32,3584]{2,1,0:T(8,128)(2,1)S(1)} %collective-permute-done.16), channel_id=1, source_target_pairs={{0,120},{8,0},{16,8},{24,16},{32,24},{40,32},{48,40},{56,48},{64,5... | collective-permute-start | bytes 1376264 | tf_op jit(solution)/shard_map/ppermute | solution.py:18
  389.1 12.0 %collective-permute-start.19 = (bf16[2,32,3584]{2,1,0:T(8,128)(2,1)S(1)}, bf16[2,32,3584]{2,1,0:T(8,128)(2,1)S(1)}, u32[]{:S(2)}, u32[]{:S(2)}) collective-permute-start(bf16[2,32,3584]{2,1,0:T(8,128)(2,1)S(1)} %collective-permute-done.17), channel_id=1, source_target_pairs={{0,8},{8,16},{16,24},{24,32},{32,40},{40,48},{48,56},{56,64},{64,7... | collective-permute-start | bytes 1376264 | tf_op jit(solution)/shard_map/ppermute | solution.py:15
  394.0 10.9 %collective-permute-start.20 = (bf16[2,32,3584]{2,1,0:T(8,128)(2,1)S(1)}, bf16[2,32,3584]{2,1,0:T(8,128)(2,1)S(1)}, u32[]{:S(2)}, u32[]{:S(2)}) collective-permute-start(bf16[2,32,3584]{2,1,0:T(8,128)(2,1)S(1)} %collective-permute-done.18), channel_id=1, source_target_pairs={{0,120},{8,0},{16,8},{24,16},{32,24},{40,32},{48,40},{56,48},{64,5... | collective-permute-start | bytes 1376264 | tf_op jit(solution)/shard_map/ppermute | solution.py:18
  401.1 10.7 %collective-permute-start.21 = (bf16[2,32,3584]{2,1,0:T(8,128)(2,1)S(1)}, bf16[2,32,3584]{2,1,0:T(8,128)(2,1)S(1)}, u32[]{:S(2)}, u32[]{:S(2)}) collective-permute-start(bf16[2,32,3584]{2,1,0:T(8,128)(2,1)S(1)} %collective-permute-done.19), channel_id=1, source_target_pairs={{0,8},{8,16},{16,24},{24,32},{32,40},{40,48},{48,56},{56,64},{64,7... | collective-permute-start | bytes 1376264 | tf_op jit(solution)/shard_map/ppermute | solution.py:15
  405.0 10.6 %collective-permute-start.22 = (bf16[2,32,3584]{2,1,0:T(8,128)(2,1)S(1)}, bf16[2,32,3584]{2,1,0:T(8,128)(2,1)S(1)}, u32[]{:S(2)}, u32[]{:S(2)}) collective-permute-start(bf16[2,32,3584]{2,1,0:T(8,128)(2,1)S(1)} %collective-permute-done.20), channel_id=1, source_target_pairs={{0,120},{8,0},{16,8},{24,16},{32,24},{40,32},{48,40},{56,48},{64,5... | collective-permute-start | bytes 1376264 | tf_op jit(solution)/shard_map/ppermute | solution.py:18
  411.9 10.7 %collective-permute-start.23 = (bf16[2,32,3584]{2,1,0:T(8,128)(2,1)S(1)}, bf16[2,32,3584]{2,1,0:T(8,128)(2,1)S(1)}, u32[]{:S(2)}, u32[]{:S(2)}) collective-permute-start(bf16[2,32,3584]{2,1,0:T(8,128)(2,1)S(1)} %collective-permute-done.21), channel_id=1, source_target_pairs={{0,8},{8,16},{16,24},{24,32},{32,40},{40,48},{48,56},{56,64},{64,7... | collective-permute-start | bytes 1376264 | tf_op jit(solution)/shard_map/ppermute | solution.py:15
  415.6 11.0 %collective-permute-start.24 = (bf16[2,32,3584]{2,1,0:T(8,128)(2,1)S(1)}, bf16[2,32,3584]{2,1,0:T(8,128)(2,1)S(1)}, u32[]{:S(2)}, u32[]{:S(2)}) collective-permute-start(bf16[2,32,3584]{2,1,0:T(8,128)(2,1)S(1)} %collective-permute-done.22), channel_id=1, source_target_pairs={{0,120},{8,0},{16,8},{24,16},{32,24},{40,32},{48,40},{56,48},{64,5... | collective-permute-start | bytes 1376264 | tf_op jit(solution)/shard_map/ppermute | solution.py:18
  422.5 11.3 %collective-permute-start.25 = (bf16[2,32,3584]{2,1,0:T(8,128)(2,1)S(1)}, bf16[2,32,3584]{2,1,0:T(8,128)(2,1)S(1)}, u32[]{:S(2)}, u32[]{:S(2)}) collective-permute-start(bf16[2,32,3584]{2,1,0:T(8,128)(2,1)S(1)} %collective-permute-done.23), channel_id=1, source_target_pairs={{0,8},{8,16},{16,24},{24,32},{32,40},{40,48},{48,56},{56,64},{64,7... | collective-permute-start | bytes 1376264 | tf_op jit(solution)/shard_map/ppermute | solution.py:15
  426.6 12.1 %collective-permute-start.26 = (bf16[2,32,3584]{2,1,0:T(8,128)(2,1)S(1)}, bf16[2,32,3584]{2,1,0:T(8,128)(2,1)S(1)}, u32[]{:S(2)}, u32[]{:S(2)}) collective-permute-start(bf16[2,32,3584]{2,1,0:T(8,128)(2,1)S(1)} %collective-permute-done.24), channel_id=1, source_target_pairs={{0,120},{8,0},{16,8},{24,16},{32,24},{40,32},{48,40},{56,48},{64,5... | collective-permute-start | bytes 1376264 | tf_op jit(solution)/shard_map/ppermute | solution.py:18
  433.8 12.4 %collective-permute-start.27 = (bf16[2,32,3584]{2,1,0:T(8,128)(2,1)S(1)}, bf16[2,32,3584]{2,1,0:T(8,128)(2,1)S(1)}, u32[]{:S(2)}, u32[]{:S(2)}) collective-permute-start(bf16[2,32,3584]{2,1,0:T(8,128)(2,1)S(1)} %collective-permute-done.25), channel_id=1, source_target_pairs={{0,8},{8,16},{16,24},{24,32},{32,40},{40,48},{48,56},{56,64},{64,7... | collective-permute-start | bytes 1376264 | tf_op jit(solution)/shard_map/ppermute | solution.py:15
  438.7 13.2 %collective-permute-start.28 = (bf16[2,32,3584]{2,1,0:T(8,128)(2,1)S(1)}, bf16[2,32,3584]{2,1,0:T(8,128)(2,1)S(1)}, u32[]{:S(2)}, u32[]{:S(2)}) collective-permute-start(bf16[2,32,3584]{2,1,0:T(8,128)(2,1)S(1)} %collective-permute-done.26), channel_id=1, source_target_pairs={{0,120},{8,0},{16,8},{24,16},{32,24},{40,32},{48,40},{56,48},{64,5... | collective-permute-start | bytes 1376264 | tf_op jit(solution)/shard_map/ppermute | solution.py:18
  446.2 13.5 %collective-permute-start.29 = (bf16[2,32,3584]{2,1,0:T(8,128)(2,1)S(1)}, bf16[2,32,3584]{2,1,0:T(8,128)(2,1)S(1)}, u32[]{:S(2)}, u32[]{:S(2)}) collective-permute-start(bf16[2,32,3584]{2,1,0:T(8,128)(2,1)S(1)} %collective-permute-done.27), channel_id=1, source_target_pairs={{0,8},{8,16},{16,24},{24,32},{32,40},{40,48},{48,56},{56,64},{64,7... | collective-permute-start | bytes 1376264 | tf_op jit(solution)/shard_map/ppermute | solution.py:15
  469.7 44.9 %reduce-scatter.16.cloned.1.call-start = ((), (), s32[]{:S(2)}) async-start(), calls=%async_computation.11 | async-start | bytes 5505024 | tf_op jit(solution)/shard_map/reduce_scatter | solution.py:118
  475.7 57.5 %reduce-scatter.14.cloned.1.call-start = ((), (), s32[]{:S(2)}) async-start(), calls=%async_computation.10 | async-start | bytes 5505024 | tf_op jit(solution)/shard_map/reduce_scatter | solution.py:112
  (14 other events, 387.8 us)
Sparse Core Ops, SparseCore 0:
  35.1 84.8 reduce-scatter.7
  200.7 26.1 reduce-scatter.9
  277.8 80.9 reduce-scatter.11
  371.3 17.1 reduce-scatter.17
  469.8 25.9 reduce-scatter.19
  498.6 15.8 reduce-scatter.15
  517.6 15.5 reduce-scatter.13
